TPU v7x, 256 devices: a whole 4x4x8 slice. The times are simulated.
256 devices in a mesh: wide: 32 (over x, z), narrow: 8 (over y, core).
Axes of the slice: x: 4, y: 4, z: 8, core: 2. Of those that a mesh axis runs over, the one named last changes fastest.
Arguments:
- tile_data: bfloat16 [81920, 128, 128], P(('wide', 'narrow')), may hold values from -0.119628906 to 0.119628906
- tile_user: int32 [81920], P(('wide', 'narrow')), may hold values from 0 to 63
- tile_item: int32 [81920], P(('wide', 'narrow')), may hold values from 0 to 31
- tile_word: int32 [81920], P(('wide', 'narrow')), may hold values from 0 to 4095
- tile_month: int32 [81920], P(('wide', 'narrow')), may hold values from 0 to 999
- tile_live: int32 [256], P(('wide', 'narrow')), may hold values from 160 to 320, as said below
- user_need: int32 [256, 64], P(('wide', 'narrow')), may hold values from 0 to 511, as said below
- item_need: int32 [256, 32], P(('wide', 'narrow')), may hold values from 0 to 511, as said below
- user_slot: int32 [512], replicated, may hold values from 0 to 511, as said below
- item_slot: int32 [512], replicated, may hold values from 0 to 511, as said below
- user_factor: bfloat16 [65536, 128], P('wide'), may hold values from -6 to 6
- word_factor: bfloat16 [4096, 128], replicated, may hold values from -6 to 6
- month_factor: bfloat16 [1000, 128], replicated, may hold values from -6 to 6
Outputs:
- item_rows: float32 [65536, 128], P(('wide', 'narrow'))
Inputs may be any that keep to these rules, and one draw needn't show every extreme that they name: user_slot is a permutation; the owner of user block b is user_slot[b] // 16. item_slot is a permutation; the owner of item block b is item_slot[b] // 16. `user_need`: entries k * 2 to k * 2 + 1 of each row are distinct user blocks whose owner is k. `item_need`: entry k of each row is an item block whose owner is k. `tile_live`: some device has all its slots live.
All inputs are finite; a program needn't handle non-finite values.
Results may differ from a plain program's by a relative error of at most 0.0029.
Values may be sent and summed in bfloat16 or wider, within the bound.
A program may use at most 128 MiB of HBM per device.

v0:
```python
import jax
import jax.numpy as jnp
from jax import lax
from jax.sharding import PartitionSpec as P


def shards(
    tile_data,
    tile_user,
    tile_item,
    tile_word,
    tile_month,
    tile_live,
    user_need,
    item_need,
    user_slot,
    item_slot,
    user_factor,
    word_factor,
    month_factor,
):
    wide_count = lax.axis_size("wide")
    tile_count = tile_data.shape[0]
    block_side = tile_data.shape[1]
    rank_width = user_factor.shape[1]
    items_owned = item_slot.shape[0] // wide_count
    touched = item_need.shape[1]
    item_local = (item_slot[item_need[0]] % items_owned).reshape(wide_count, -1)
    item_from = lax.all_to_all(item_local, "wide", split_axis=0, concat_axis=0, tiled=True)
    user_place = user_slot[user_need[0]]
    gathered = lax.all_gather(user_factor, "wide", axis=0, tiled=True)
    fetched = gathered.reshape(-1, block_side, rank_width)[user_place]
    word_month = word_factor[tile_word].astype(jnp.float32) * month_factor[tile_month].astype(
        jnp.float32
    )
    scaled = (fetched[tile_user].astype(jnp.float32) * word_month[:, None, :]).astype(jnp.bfloat16)
    contrib = jnp.einsum("tab,tar->tbr", tile_data, scaled, preferred_element_type=jnp.float32)
    is_live = lax.iota(jnp.int32, tile_count) < tile_live[0]
    group_ids = jnp.where(is_live, tile_item, touched)
    partial_value = jax.ops.segment_sum(contrib, group_ids, num_segments=touched + 1)[:touched]
    arrived = lax.all_to_all(
        partial_value.reshape(wide_count, -1, block_side, rank_width),
        "wide",
        split_axis=0,
        concat_axis=0,
        tiled=True,
    )
    arrived = arrived.reshape(-1, block_side, rank_width)
    slot_ids = item_from.reshape(-1)
    placing = (slot_ids[:, None] == lax.iota(jnp.int32, items_owned)[None, :]).astype(jnp.float32)
    owner_sum = jnp.einsum("kj,kbr->jbr", placing, arrived, precision=lax.Precision.HIGHEST)
    owned_rows = lax.psum_scatter(owner_sum, "narrow", scatter_dimension=0, tiled=True)
    return owned_rows.reshape(-1, rank_width)


def solution(mesh):
    return jax.shard_map(
        shards,
        mesh=mesh,
        in_specs=(
            P(("wide", "narrow"), None, None),
            P(("wide", "narrow")),
            P(("wide", "narrow")),
            P(("wide", "narrow")),
            P(("wide", "narrow")),
            P(("wide", "narrow")),
            P(("wide", "narrow"), None),
            P(("wide", "narrow"), None),
            P(),
            P(),
            P("wide", None),
            P(),
            P(),
        ),
        out_specs=P(("wide", "narrow"), None),
        check_vma=False,
    )
```

profile of v0, /device:TPU:4, one launch (start us, length us, event | category | flops | bytes accessed | tf_op | source)
XLA Modules:
  0.0 346.2 jit_solution(6248891772234273754)
XLA Ops:
  6.5 0.0 copy-start
  6.5 0.0 all-gather.2.cloned.1.call-start
  6.5 0.7 all-gather.2.cloned.1.call-update
  7.3 0.7 fusion.11
  7.9 1.4 gather_fusion
  9.3 0.7 copy.26
  10.0 11.6 %all-to-all-start = ((s32[32,1,1]{2,1,0:T(1,128)}), s32[32,1,1]{2,1,0:T(1,128)S(1)}, u32[]{:S(2)}, u32[]{:S(2)}) async-start(s32[32,1,1]{2,1,0:T(1,128)} %copy.26), calls=%async_computation | async-start | bytes 32768 | tf_op jit(solution)/shard_map/all_to_all | solution.py:29
  22.3 0.7 fusion.12
  22.9 1.5 gather_fusion.1
  24.4 0.7 compare_select_fusion.1
  25.1 0.0 copy-done
  25.1 1.4 gather_fusion.4
  26.5 0.7 compare_select_fusion
  27.2 2.1 gather_fusion.5
  29.4 0.7 compare_select_fusion.2
  30.1 0.7 fusion.9
  30.8 121.1 %all-gather.2.cloned.1.call-done = bf16[65536,128]{1,0:T(8,128)(2,1)} async-done(((bf16[2048,128]{1,0:T(8,128)(2,1)}), bf16[65536,128]{1,0:T(8,128)(2,1)}) %all-gather.2.cloned.1.call-update) | async-done | bytes 16777232 | tf_op jit(solution)/shard_map/all_gather | solution.py:31
  151.9 6.7 %gather_fusion.2 = bf16[64,128,128]{2,1,0:T(8,128)(2,1)S(1)} fusion(bf16[512,128,128]{2,1,0:T(8,128)(2,1)} %bitcast.31, s32[1024]{0:T(1024)S(1)} %pad_clamp_fusion.3), kind=kCustom, calls=%fused_computation.2 | custom fusion | bytes 4194560 | tf_op jit(solution)/shard_map/gather | solution.py:32
  158.6 10.7 %gather_fusion.3 = bf16[320,128,128]{2,1,0:T(8,128)(2,1)} fusion(bf16[64,128,128]{2,1,0:T(8,128)(2,1)S(1)} %gather_fusion.2, s32[1024]{0:T(1024)S(1)} %pad_clamp_fusion.2), kind=kCustom, calls=%fused_computation.3 | custom fusion | bytes 20972800 | tf_op jit(solution)/shard_map/gather | solution.py:36
  169.3 12.9 %fusion.2 = f32[320,128,128]{1,2,0:T(8,128)} fusion(bf16[320,128,128]{2,1,0:T(8,128)(2,1)} %param.13, bf16[320,128,128]{2,1,0:T(8,128)(2,1)} %gather_fusion.3, f32[320,128]{1,0:T(8,128)S(1)} %convert_multiply_fusion), kind=kOutput, calls=%fused_computation.10 | convolution fusion | flops 1357905920 | bytes 42106880 | tf_op jit(solution)/shard_map/tab,tar->tbr/dot_general | solution.py:37
  182.3 21.1 %copy.28 = f32[320,128,128]{2,1,0:T(8,128)} copy(f32[320,128,128]{1,2,0:T(8,128)} %fusion.2) | data formatting | bytes 41943040 | tf_op jit(solution)/shard_map/tab,tar->tbr/dot_general | solution.py:37
  203.4 0.2 broadcast_in_dim.24
  203.7 0.0 copy-start.1
  203.7 41.9 %scatter_fusion = f32[33,128,128]{2,1,0:T(8,128)S(1)} fusion(f32[33,128,128]{2,1,0:T(8,128)S(1)} %broadcast_in_dim.24, s32[320]{0:T(512)S(1)} %fusion.9, f32[320,128,128]{2,1,0:T(8,128)} %copy.28), kind=kCustom, calls=%fused_computation.6 | custom fusion | flops 5242880 | bytes 62915840 | tf_op jit(solution)/shard_map/scatter-add | solution.py:40
  245.6 1.5 slice_bitcast_fusion
  247.1 0.0 all-to-all-done
  247.1 7.5 %all-to-all-start.1 = ((f32[32,1,128,128]{3,2,1,0:T(8,128)}), f32[32,1,128,128]{3,2,1,0:T(8,128)S(1)}, u32[]{:S(2)}, u32[]{:S(2)}) async-start(f32[32,1,128,128]{3,2,1,0:T(8,128)} %slice_bitcast_fusion), calls=%async_computation.1 | async-start | bytes 4194304 | tf_op jit(solution)/shard_map/all_to_all | solution.py:41
  254.5 0.0 reduce-scatter.2.cloned.1.call-start
  254.6 0.7 reduce
  255.2 46.4 %all-to-all-done.1 = f32[32,1,128,128]{3,2,1,0:T(8,128)S(1)} async-done(((f32[32,1,128,128]{3,2,1,0:T(8,128)}), f32[32,1,128,128]{3,2,1,0:T(8,128)S(1)}, u32[]{:S(2)}, u32[]{:S(2)}) %all-to-all-start.1) | async-done | bytes 2097184 | tf_op jit(solution)/shard_map/all_to_all | solution.py:41
  301.7 2.0 fusion.3
  303.7 1.3 copy.31
  305.0 0.0 reduce-scatter.2.cloned.1.call-update
  305.0 34.4 %reduce-scatter.2.cloned.1.call-done = f32[2,128,128]{2,1,0:T(8,128)} async-done(((f32[16,128,128]{2,1,0:T(8,128)}), f32[2,128,128]{2,1,0:T(8,128)}) %reduce-scatter.2.cloned.1.call-update) | async-done | bytes 131088 | tf_op jit(solution)/shard_map/reduce_scatter | solution.py:52
  339.4 0.0 copy-done.1
  (9 shorter events, 0.1 us)
Async XLA Ops:
  6.5 18.6 %copy-start = (bf16[4096,128]{1,0:T(8,128)(2,1)S(1)}, bf16[4096,128]{1,0:T(8,128)(2,1)}, u32[]{:S(2)}) copy-start(bf16[4096,128]{1,0:T(8,128)(2,1)} %param.24) | copy-start | bytes 3145732
  6.5 145.3 %all-gather.2.cloned.1.call-start = ((), (), s32[]{:S(2)}) async-start(), calls=%async_computation.3 | async-start | bytes 17301504 | tf_op jit(solution)/shard_map/all_gather | solution.py:31
  10.0 237.0 %all-to-all-start = ((s32[32,1,1]{2,1,0:T(1,128)}), s32[32,1,1]{2,1,0:T(1,128)S(1)}, u32[]{:S(2)}, u32[]{:S(2)}) async-start(s32[32,1,1]{2,1,0:T(1,128)} %copy.26), calls=%async_computation | async-start | bytes 32768 | tf_op jit(solution)/shard_map/all_to_all | solution.py:29
  203.7 135.7 %copy-start.1 = (bf16[4096,128]{1,0:T(8,128)(2,1)S(1)}, bf16[4096,128]{1,0:T(8,128)(2,1)}, u32[]{:S(2)}) copy-start(bf16[4096,128]{1,0:T(8,128)(2,1)} %param.24) | copy-start | bytes 3145732
  247.1 54.6 %all-to-all-start.1 = ((f32[32,1,128,128]{3,2,1,0:T(8,128)}), f32[32,1,128,128]{3,2,1,0:T(8,128)S(1)}, u32[]{:S(2)}, u32[]{:S(2)}) async-start(f32[32,1,128,128]{3,2,1,0:T(8,128)} %slice_bitcast_fusion), calls=%async_computation.1 | async-start | bytes 4194304 | tf_op jit(solution)/shard_map/all_to_all | solution.py:41
  254.5 84.8 %reduce-scatter.2.cloned.1.call-start = ((), (), s32[]{:S(2)}) async-start(), calls=%async_computation.4 | async-start | bytes 1179648 | tf_op jit(solution)/shard_map/reduce_scatter | solution.py:52
Sparse Core Ops, SparseCore 0:
  10.0 141.8 all-gather.1
  305.1 34.2 reduce-scatter.1
where the time goes:
time: 348 us; the launch traced here: 346 us
  waiting for transfers between devices  203 us (58%)
  local copies, waits for them, and re-layouts  48.7 us (14%)
  other arithmetic  46.7 us (13%)
  starting transfers between devices  19.1 us (5%)
  matrix products  14.9 us (4%)
  between operations  14.1 us (4%)
    all_gather x1, waiting for transfers between devices, shards(): gathered = lax.all_gather(user_factor, 'wide', axis=0, tiled=True)  121 us
    all_to_all x1, waiting for transfers between devices, shards(): lax.all_to_all(partial_value.reshape(wide_count, -1, block_side, rank_wid...  46.4 us
    scatter-add x1, other arithmetic, shards(): jax.ops.segment_sum(contrib, group_ids, num_segments=touched + 1)[:touched]  41.9 us
    reduce_scatter x1, waiting for transfers between devices, shards(): lax.psum_scatter(owner_sum, 'narrow', scatter_dimension=0, tiled=True)  34.4 us
    dot_general x1, local copies, waits for them, and re-layouts, shards(): jnp.einsum('tab,tar->tbr', tile_data, scaled, preferred_element_type=jnp....  21.1 us
    dot_general x1, matrix products, shards(): jnp.einsum('tab,tar->tbr', tile_data, scaled, preferred_element_type=jnp....  12.9 us
    all_to_all x1, starting transfers between devices, shards(): lax.all_to_all(item_local, 'wide', split_axis=0, concat_axis=0, tiled=True)  11.6 us
    gather x1, local copies, waits for them, and re-layouts, shards(): fetched[tile_user].astype(jnp.float32) * word_month[:, None, :]  10.7 us
  transfers between devices with their start and end apart: 4, of which 3 were waited for; matrix products, arithmetic and copies ran while one was open for 31% of the time, Pallas kernels for 0%

commit v1 on v0

--- a/solution.py
+++ b/solution.py
@@ -28,7 +28,10 @@
     item_local = (item_slot[item_need[0]] % items_owned).reshape(wide_count, -1)
     item_from = lax.all_to_all(item_local, "wide", split_axis=0, concat_axis=0, tiled=True)
     user_place = user_slot[user_need[0]]
-    gathered = lax.all_gather(user_factor, "wide", axis=0, tiled=True)
+    size = lax.axis_size("wide")
+    tiles = jnp.stack([user_factor for _ in range(size)])
+    tiles = lax.all_to_all(tiles, "wide", split_axis=0, concat_axis=0)
+    gathered = jnp.concatenate(tiles, axis=0)
     fetched = gathered.reshape(-1, block_side, rank_width)[user_place]
     word_month = word_factor[tile_word].astype(jnp.float32) * month_factor[tile_month].astype(
         jnp.float32

time: 348 us -> 639 us (1.84)
  waiting for transfers between devices: 203 us -> 457 us
  starting transfers between devices: 19.1 us -> 55.1 us
    all_to_all x0 -> x1, waiting for transfers between devices: none -> 377 us  [shards(): tiles = lax.all_to_all(tiles, 'wide', split_axis=0, concat_axis=0)]
    all_gather x1 -> x0, waiting for transfers between devices: 121 us -> none  [shards(): gathered = lax.all_gather(user_factor, 'wide', axis=0, tiled=True)]
    all_to_all x1, starting transfers between devices: 11.6 us -> 33.3 us  [shards(): lax.all_to_all(item_local, 'wide', split_axis=0, concat_axis=0, tiled=True)]
    all_to_all x0 -> x1, starting transfers between devices: none -> 11.8 us  [shards(): tiles = lax.all_to_all(tiles, 'wide', split_axis=0, concat_axis=0)]
    another operation x0 -> x1, local copies, waits for them, and re-layouts: none -> 7.07 us  [shards(): tiles = jnp.stack([user_factor for _ in range(size)])]
  transfers between devices with their start and end apart: 4 -> 4, of which waited for: 3 -> 3; matrix products, arithmetic and copies ran while one was open for 31% -> 16% of each run, Pallas kernels for 0% -> 0%
where the time goes in v1:
time: 639 us; the launch traced here: 637 us
  waiting for transfers between devices  457 us (72%)
  starting transfers between devices  55.1 us (9%)
  local copies, waits for them, and re-layouts  53.7 us (8%)
  other arithmetic  42.7 us (7%)
  matrix products  14.9 us (2%)
  between operations  14.3 us (2%)
    all_to_all x1, waiting for transfers between devices, shards(): tiles = lax.all_to_all(tiles, 'wide', split_axis=0, concat_axis=0)  377 us
    all_to_all x1, waiting for transfers between devices, shards(): lax.all_to_all(partial_value.reshape(wide_count, -1, block_side, rank_wid...  45.4 us
    scatter-add x1, other arithmetic, shards(): jax.ops.segment_sum(contrib, group_ids, num_segments=touched + 1)[:touched]  41.9 us
    reduce_scatter x1, waiting for transfers between devices, shards(): lax.psum_scatter(owner_sum, 'narrow', scatter_dimension=0, tiled=True)  34.1 us
    all_to_all x1, starting transfers between devices, shards(): lax.all_to_all(item_local, 'wide', split_axis=0, concat_axis=0, tiled=True)  33.3 us
    dot_general x1, local copies, waits for them, and re-layouts, shards(): jnp.einsum('tab,tar->tbr', tile_data, scaled, preferred_element_type=jnp....  21.1 us
    dot_general x1, matrix products, shards(): jnp.einsum('tab,tar->tbr', tile_data, scaled, preferred_element_type=jnp....  12.9 us
  transfers between devices with their start and end apart: 4, of which 3 were waited for; matrix products, arithmetic and copies ran while one was open for 16% of the time, Pallas kernels for 0%

profile of v1, /device:TPU:4, one launch (start us, length us, event | category | flops | bytes accessed | tf_op | source)
XLA Modules:
  0.0 637.3 jit_solution(7277944701398943559)
XLA Ops:
  6.5 0.0 copy-start
  6.5 7.1 %stack.2 = bf16[32,2048,128]{2,1,0:T(8,128)(2,1)} broadcast(bf16[2048,128]{1,0:T(8,128)(2,1)} %param.23), dimensions={1,2} | broadcast | bytes 17301504 | tf_op jit(solution)/shard_map/stack | solution.py:32
  13.6 0.0 copy-start.9
  13.6 0.0 copy-start.2
  13.6 0.0 copy-start.10
  13.6 0.0 copy-start.3
  13.6 0.0 copy-start.5
  13.6 0.0 copy-start.6
  13.7 0.0 copy-start.4
  13.7 0.0 copy-start.7
  13.7 0.0 copy-start.8
  13.7 11.8 %all-to-all-start.1 = ((bf16[32,2048,128]{2,1,0:T(8,128)(2,1)}), bf16[32,2048,128]{2,1,0:T(8,128)(2,1)}, u32[]{:S(2)}, u32[]{:S(2)}) async-start(bf16[32,2048,128]{2,1,0:T(8,128)(2,1)} %stack.2), calls=%async_computation.1 | async-start | bytes 33554432 | tf_op jit(solution)/shard_map/all_to_all | solution.py:33
  26.1 0.0 copy-done.9
  26.2 0.0 copy-done.2
  26.2 0.7 gather_fusion
  26.9 0.7 copy.26
  27.6 0.0 copy-done.10
  27.6 0.0 copy-done.3
  27.6 0.8 gather_fusion.1
  28.4 0.0 copy-done.5
  28.4 0.0 copy-done
  28.5 1.4 gather_fusion.4
  29.9 0.0 copy-done.6
  29.9 0.0 copy-done.4
  29.9 1.4 gather_fusion.5
  31.3 0.0 copy-done.7
  31.4 0.0 copy-done.8
  31.4 377.0 %all-to-all-done.1 = bf16[32,2048,128]{2,1,0:T(8,128)(2,1)} async-done(((bf16[32,2048,128]{2,1,0:T(8,128)(2,1)}), bf16[32,2048,128]{2,1,0:T(8,128)(2,1)}, u32[]{:S(2)}, u32[]{:S(2)}) %all-to-all-start.1) | async-done | bytes 16777248 | tf_op jit(solution)/shard_map/all_to_all | solution.py:33
  408.4 33.3 %all-to-all-start = ((s32[32,1,1]{2,1,0:T(1,128)}), s32[32,1,1]{2,1,0:T(1,128)S(1)}, u32[]{:S(2)}, u32[]{:S(2)}) async-start(s32[32,1,1]{2,1,0:T(1,128)} %copy.26), calls=%async_computation | async-start | bytes 32768 | tf_op jit(solution)/shard_map/all_to_all | solution.py:29
  441.8 6.7 %gather_fusion.2 = bf16[64,128,128]{2,1,0:T(8,128)(2,1)S(1)} fusion(bf16[512,128,128]{2,1,0:T(8,128)(2,1)} %bitcast.5, s32[1024]{0:T(1024)S(1)} %pad_clamp_fusion.3), kind=kCustom, calls=%fused_computation.2 | custom fusion | bytes 4194560 | tf_op jit(solution)/shard_map/gather | solution.py:35
  448.5 10.7 %gather_fusion.3 = bf16[320,128,128]{2,1,0:T(8,128)(2,1)} fusion(bf16[64,128,128]{2,1,0:T(8,128)(2,1)S(1)} %gather_fusion.2, s32[1024]{0:T(1024)S(1)} %pad_clamp_fusion.2), kind=kCustom, calls=%fused_computation.3 | custom fusion | bytes 20972800 | tf_op jit(solution)/shard_map/gather | solution.py:39
  459.2 12.9 %fusion.2 = f32[320,128,128]{1,2,0:T(8,128)} fusion(bf16[320,128,128]{2,1,0:T(8,128)(2,1)} %param.13, bf16[320,128,128]{2,1,0:T(8,128)(2,1)} %gather_fusion.3, f32[320,128]{1,0:T(8,128)S(1)} %convert_multiply_fusion), kind=kOutput, calls=%fused_computation.10 | convolution fusion | flops 1357905920 | bytes 42106880 | tf_op jit(solution)/shard_map/tab,tar->tbr/dot_general | solution.py:40
  472.2 21.1 %copy.28 = f32[320,128,128]{2,1,0:T(8,128)} copy(f32[320,128,128]{1,2,0:T(8,128)} %fusion.2) | data formatting | bytes 41943040 | tf_op jit(solution)/shard_map/tab,tar->tbr/dot_general | solution.py:40
  493.3 0.2 broadcast_in_dim.24
  493.6 0.0 copy-start.1
  493.6 41.9 %scatter_fusion = f32[33,128,128]{2,1,0:T(8,128)S(1)} fusion(f32[33,128,128]{2,1,0:T(8,128)S(1)} %broadcast_in_dim.24, s32[320]{0:T(512)S(1)} %fusion.9, f32[320,128,128]{2,1,0:T(8,128)} %copy.28), kind=kCustom, calls=%fused_computation.6 | custom fusion | flops 5242880 | bytes 62915840 | tf_op jit(solution)/shard_map/scatter-add | solution.py:43
  535.5 1.5 slice_bitcast_fusion
  537.0 0.0 all-to-all-done
  537.0 9.8 %all-to-all-start.2 = ((f32[32,1,128,128]{3,2,1,0:T(8,128)}), f32[32,1,128,128]{3,2,1,0:T(8,128)S(1)}, u32[]{:S(2)}, u32[]{:S(2)}) async-start(f32[32,1,128,128]{3,2,1,0:T(8,128)} %slice_bitcast_fusion), calls=%async_computation.2 | async-start | bytes 4194304 | tf_op jit(solution)/shard_map/all_to_all | solution.py:44
  546.7 0.2 reduce-scatter.2.cloned.1.call-start
  547.0 0.7 reduce
  547.6 45.4 %all-to-all-done.2 = f32[32,1,128,128]{3,2,1,0:T(8,128)S(1)} async-done(((f32[32,1,128,128]{3,2,1,0:T(8,128)}), f32[32,1,128,128]{3,2,1,0:T(8,128)S(1)}, u32[]{:S(2)}, u32[]{:S(2)}) %all-to-all-start.2) | async-done | bytes 2097184 | tf_op jit(solution)/shard_map/all_to_all | solution.py:44
  593.0 2.0 fusion.3
  595.0 1.3 copy.31
  596.3 0.0 reduce-scatter.2.cloned.1.call-update
  596.4 34.1 %reduce-scatter.2.cloned.1.call-done = f32[2,128,128]{2,1,0:T(8,128)} async-done(((f32[16,128,128]{2,1,0:T(8,128)}), f32[2,128,128]{2,1,0:T(8,128)}) %reduce-scatter.2.cloned.1.call-update) | async-done | bytes 131088 | tf_op jit(solution)/shard_map/reduce_scatter | solution.py:55
  630.5 0.0 copy-done.1
  (15 shorter events, 0.1 us)
Async XLA Ops:
  6.5 21.9 %copy-start = (bf16[4096,128]{1,0:T(8,128)(2,1)S(1)}, bf16[4096,128]{1,0:T(8,128)(2,1)}, u32[]{:S(2)}) copy-start(bf16[4096,128]{1,0:T(8,128)(2,1)} %param.24) | copy-start | bytes 3145732
  13.6 12.5 %copy-start.9 = (s32[1,32]{1,0:T(1,128)S(1)}, s32[1,32]{1,0:T(1,128)}, u32[]{:S(2)}) copy-start(s32[1,32]{1,0:T(1,128)} %param.20) | copy-start | bytes 388
  13.6 12.6 %copy-start.2 = (s32[512]{0:T(512)S(1)}, s32[512]{0:T(512)}, u32[]{:S(2)}) copy-start(s32[512]{0:T(512)} %param.22) | copy-start | bytes 6148
  13.6 14.0 %copy-start.10 = (s32[1,64]{1,0:T(1,128)S(1)}, s32[1,64]{1,0:T(1,128)}, u32[]{:S(2)}) copy-start(s32[1,64]{1,0:T(1,128)} %param.19) | copy-start | bytes 772
  13.6 14.0 %copy-start.3 = (s32[512]{0:T(512)S(1)}, s32[512]{0:T(512)}, u32[]{:S(2)}) copy-start(s32[512]{0:T(512)} %param.21) | copy-start | bytes 6148
  13.6 14.8 %copy-start.5 = (s32[320]{0:T(512)S(1)}, s32[320]{0:T(512)}, u32[]{:S(2)}) copy-start(s32[320]{0:T(512)} %param.16) | copy-start | bytes 3844
  13.6 16.2 %copy-start.6 = (s32[320]{0:T(512)S(1)}, s32[320]{0:T(512)}, u32[]{:S(2)}) copy-start(s32[320]{0:T(512)} %param.17) | copy-start | bytes 3844
  13.7 16.3 %copy-start.4 = (bf16[1000,128]{1,0:T(8,128)(2,1)S(1)}, bf16[1000,128]{1,0:T(8,128)(2,1)}, u32[]{:S(2)}) copy-start(bf16[1000,128]{1,0:T(8,128)(2,1)} %param.25) | copy-start | bytes 768004
  13.7 17.7 %copy-start.7 = (s32[320]{0:T(512)S(1)}, s32[320]{0:T(512)}, u32[]{:S(2)}) copy-start(s32[320]{0:T(512)} %param.14) | copy-start | bytes 3844
  13.7 17.7 %copy-start.8 = (s32[320]{0:T(512)S(1)}, s32[320]{0:T(512)}, u32[]{:S(2)}) copy-start(s32[320]{0:T(512)} %param.15) | copy-start | bytes 3844
  13.7 394.7 %all-to-all-start.1 = ((bf16[32,2048,128]{2,1,0:T(8,128)(2,1)}), bf16[32,2048,128]{2,1,0:T(8,128)(2,1)}, u32[]{:S(2)}, u32[]{:S(2)}) async-start(bf16[32,2048,128]{2,1,0:T(8,128)(2,1)} %stack.2), calls=%async_computation.1 | async-start | bytes 33554432 | tf_op jit(solution)/shard_map/all_to_all | solution.py:33
  408.4 128.5 %all-to-all-start = ((s32[32,1,1]{2,1,0:T(1,128)}), s32[32,1,1]{2,1,0:T(1,128)S(1)}, u32[]{:S(2)}, u32[]{:S(2)}) async-start(s32[32,1,1]{2,1,0:T(1,128)} %copy.26), calls=%async_computation | async-start | bytes 32768 | tf_op jit(solution)/shard_map/all_to_all | solution.py:29
  493.6 136.9 %copy-start.1 = (bf16[4096,128]{1,0:T(8,128)(2,1)S(1)}, bf16[4096,128]{1,0:T(8,128)(2,1)}, u32[]{:S(2)}) copy-start(bf16[4096,128]{1,0:T(8,128)(2,1)} %param.24) | copy-start | bytes 3145732
  537.0 56.1 %all-to-all-start.2 = ((f32[32,1,128,128]{3,2,1,0:T(8,128)}), f32[32,1,128,128]{3,2,1,0:T(8,128)S(1)}, u32[]{:S(2)}, u32[]{:S(2)}) async-start(f32[32,1,128,128]{3,2,1,0:T(8,128)} %slice_bitcast_fusion), calls=%async_computation.2 | async-start | bytes 4194304 | tf_op jit(solution)/shard_map/all_to_all | solution.py:44
  546.7 83.7 %reduce-scatter.2.cloned.1.call-start = ((), (), s32[]{:S(2)}) async-start(), calls=%async_computation.4 | async-start | bytes 1179648 | tf_op jit(solution)/shard_map/reduce_scatter | solution.py:55
Sparse Core Ops, SparseCore 0:
  596.5 33.9 reduce-scatter.1
